TPU v7x, 32 devices: a whole 2x2x4 slice. The times are simulated.
32 devices in a mesh: runs: 2 (over x), brick: 16 (over z, y, core).
Axes of the slice: x: 2, y: 2, z: 4, core: 2. Of those that a mesh axis runs over, the one named last changes fastest.
Arguments:
- grid: float32 [3, 8388608], P(None, ('runs', 'brick')), parts along dimension 1, may hold values from 0.2 to 4
- distribution: float32 [64, 16384], P(None, ('runs', 'brick')), parts along dimension 1, may hold values from 0.02 to 1
- owner_ids: int32 [16384, 1], P(('runs', 'brick')), parts along dimension 0, may hold values from 0 to 15; in each aligned block of 512 rows (0 to 511, 512 to 1023, ...) at most 64 rows name the same one
- coords: int32 [3, 16384], P(None, ('runs', 'brick')), parts along dimension 1, may hold values from 0 to 62
- fracs: float32 [3, 16384], P(None, ('runs', 'brick')), parts along dimension 1, may hold values from 0 to 1
- counts: int32 [16384], P(('runs', 'brick')), parts along dimension 0, may hold values from 1 to 4
- kernel: float32 [64, 64], replicated, may hold values from 0.002 to 0.2
- redist: float32 [64, 64], replicated, may hold values from 0.001 to 0.05
- shatter: float32 [64, 64], replicated, may hold values from 0.001 to 0.05
Outputs:
- updated: float32 [64, 16384], P(None, ('runs', 'brick')), parts along dimension 1
There are 2 independent parts, one for each index of `runs`. A program takes and returns all parts, laid end to end along the dimension named above; an argument that names none is the same for every part. Nothing has to cross between parts.
Inputs may be any that keep to these rules, and one draw needn't show every extreme that they name: `owner_ids`: in the rows of one device at most 64 tracers name one brick, a bound that some block reaches of them.
All inputs are finite; a program needn't handle non-finite values.
Results may differ from a plain program's by a relative error of at most 0.0001.
Values sent between devices are 32-bit elements; how exact they have to be, the bound alone decides.
A program may use at most 256 MiB of HBM per device.

v0:
```python
import jax
import jax.numpy as jnp
from jax import lax
from jax.sharding import PartitionSpec as P

BS = 64


def corner_sum(fields, coords, fracs, side, offset):
    total = jnp.zeros(fracs.shape, jnp.float32)
    for corner in range(8):
        first = corner // 4
        second = corner // 2 % 2
        third = corner % 2
        weight = jnp.ones(fracs.shape[1:], jnp.float32)
        weight = weight * (fracs[0] if first else 1.0 - fracs[0])
        weight = weight * (fracs[1] if second else 1.0 - fracs[1])
        weight = weight * (fracs[2] if third else 1.0 - fracs[2])
        where = (
            ((coords[0] + first) * side + coords[1] + second) * side + coords[2] + third + offset
        )
        picked = jnp.take(fields, where.astype(jnp.int32), axis=1)
        total = total + weight[None] * picked
    return total


def advance(dist, coag, shat, steps, kernel, redist, shatter):
    step_size = 1.0 / jnp.maximum(steps, 1).astype(jnp.float32)
    for section in range(4):
        kernel_dot = jnp.einsum("ij,j...->i...", kernel, dist, precision=lax.Precision.HIGHEST)
        collided = dist * kernel_dot
        gain = coag * jnp.einsum("ij,j...->i...", redist, collided, precision=lax.Precision.HIGHEST)
        gain = gain + shat * jnp.einsum(
            "ij,j...->i...", shatter, dist, precision=lax.Precision.HIGHEST
        )
        loss = coag * kernel_dot + shat
        fresh = (dist + step_size * gain) / (1.0 + step_size * loss)
        dist = jnp.where(steps >= section + 1, fresh, dist)
    return dist


def slot_of(owner, bricks, capacity):
    order = jnp.argsort(owner, stable=True)
    onehot = (owner[:, None] == jnp.arange(bricks, dtype=jnp.int32)[None, :]).astype(jnp.int32)
    per_brick = jnp.sum(onehot, axis=0)
    starts = jnp.cumsum(per_brick) - per_brick
    ranked = jnp.arange(owner.shape[0], dtype=jnp.int32) - starts[owner[order]]
    rank = jnp.zeros_like(owner).at[order].set(ranked)
    return owner * capacity + rank


def packed(values, slot, bricks, capacity):
    lead = values.shape[0]
    buffer = jnp.zeros((lead, bricks * capacity), values.dtype).at[:, slot].set(values)
    return buffer.reshape(lead, bricks, capacity)


def shards(grid, distribution, owner_ids, coords, fracs, counts, kernel, redist, shatter):
    bricks = lax.axis_size("brick")
    tracer_count = distribution.shape[1]
    capacity = 2 * tracer_count // bricks
    owner = owner_ids[:, 0]
    slot = slot_of(owner, bricks, capacity)
    sent_coords = packed(coords, slot, bricks, capacity)
    sent_fracs = packed(fracs, slot, bricks, capacity)
    local_coords = lax.all_to_all(sent_coords, "brick", split_axis=1, concat_axis=1, tiled=True)
    local_fracs = lax.all_to_all(sent_fracs, "brick", split_axis=1, concat_axis=1, tiled=True)
    values = corner_sum(grid, local_coords, local_fracs, BS, 0)
    returned = lax.all_to_all(values, "brick", split_axis=1, concat_axis=1, tiled=True)
    sampled = returned.reshape(3, bricks * capacity)[:, slot]
    coag = sampled[0] * jnp.sqrt(sampled[1])
    shat = sampled[2] * sampled[1]
    return advance(distribution, coag, shat, counts, kernel, redist, shatter)


def solution(mesh):
    in_specs = (
        P(None, ("runs", "brick")),
        P(None, ("runs", "brick")),
        P(("runs", "brick"), None),
        P(None, ("runs", "brick")),
        P(None, ("runs", "brick")),
        P(("runs", "brick")),
        P(),
        P(),
        P(),
    )
    out_specs = P(None, ("runs", "brick"))
    return jax.shard_map(shards, mesh=mesh, in_specs=in_specs, out_specs=out_specs, check_vma=False)
```

profile of v0, /device:TPU:0, one launch (start us, length us, event | category | flops | bytes accessed | tf_op | source)
XLA Modules:
  0.0 407.8 jit_solution(16366500062241387560)
XLA Ops:
  0.0 0.8 convert_reduce_fusion
  1.1 0.7 fusion.45
  1.8 4.4 %sort.17 = (s32[512]{0:T(512)}, s32[512]{0:T(512)S(1)}) sort(s32[512]{0:T(512)} %bitcast.222, s32[512]{0:T(512)S(1)} %iota.11), dimensions={0}, to_apply=%region_0.0 | sort | flops 4608 | bytes 8192 | tf_op jit(solution)/shard_map/jit(argsort)/sort | solution.py:43
  6.3 3.6 gather_fusion
  9.9 4.4 %compare_select_fusion.9 = (s32[512,1]{0,1:T(1,128)S(1)}, s32[512,1]{0,1:T(1,128)S(1)}) fusion(s32[]{:T(128)} %bitcast.12, s32[]{:T(128)} %bitcast.13, s32[]{:T(128)} %bitcast.14, s32[]{:T(128)} %bitcast.15, s32[]{:T(128)} %bitcast.16, s32[]{:T(128)} %bitcast.18, s32[]{:T(128)} %bitcast.17, s32[512,1]{0,1:T(1,128)S(1)} %bitcast.252), kind=kLoop, calls=%fused_computation.121 | loop fusion | flops 7680 | bytes 6172 | tf_op jit(solution)/shard_map/gather | solution.py:47
  14.4 5.5 %select_subtract_fusion = s32[512]{0:T(512)S(1)} fusion(pred[512]{0:T(512)(128)(4,1)S(1)} %get-tuple-element.18, pred[512]{0:T(512)(128)(4,1)S(1)} %get-tuple-element.17, pred[512]{0:T(512)(128)(4,1)S(1)} %get-tuple-element.16, pred[512]{0:T(512)(128)(4,1)S(1)} %get-tuple-element.15, pred[512]{0:T(512)(128)(4,1)S(1)} %get-tuple-element.14, ...), kind=kLoop, calls=%fused_computation.142 | loop fusion | flops 5120 | bytes 8740 | tf_op jit(solution)/shard_map/sub | solution.py:47
  19.9 2.4 scatter_custom_fusion
  22.4 0.7 compare_select_fusion.15
  23.1 0.8 copy.74
  23.9 1.8 scatter_custom_fusion.2
  26.0 0.7 reshape.326
  26.7 7.4 %all-to-all-start.1 = ((s32[16,1,192]{2,1,0:T(1,128)}), s32[16,1,192]{2,1,0:T(1,128)S(1)}, u32[]{:S(2)}, u32[]{:S(2)}) async-start(s32[16,1,192]{2,1,0:T(1,128)} %reshape.326), calls=%async_computation.1 | async-start | bytes 32768 | tf_op jit(solution)/shard_map/all_to_all | solution.py:66
  34.1 0.7 broadcast_compare_fusion.3
  34.8 1.2 fusion.47
  36.0 0.7 convert_divide_fusion
  36.7 58.6 %copy.79 = f32[3,262144]{0,1:T(8,128)} copy(f32[3,262144]{1,0:T(4,128)} %param.11) | data formatting | bytes 6291456 | tf_op args[0]
  95.4 1.8 scatter_custom_fusion.1
  97.5 0.7 reshape.328
  98.2 6.0 %all-to-all-start = ((f32[16,1,192]{2,1,0:T(1,128)}), f32[16,1,192]{2,1,0:T(1,128)S(1)}, u32[]{:S(2)}, u32[]{:S(2)}) async-start(f32[16,1,192]{2,1,0:T(1,128)} %reshape.328), calls=%async_computation | async-start | bytes 32768 | tf_op jit(solution)/shard_map/all_to_all | solution.py:67
  104.2 0.5 broadcast.418
  104.7 0.7 reduce.23
  106.2 33.6 %gather_fusion.2 = f32[1024,3]{1,0:T(8,128)S(1)} fusion(f32[3,262144]{0,1:T(8,128)} %copy.79, s32[1024]{0:T(1024)S(1)} %broadcast_clamp_fusion.7), kind=kCustom, calls=%fused_computation.clone | custom fusion | bytes 28672 | tf_op jit(solution)/shard_map/jit(_take)/gather | solution.py:22
  140.0 32.9 %gather_fusion.3 = f32[1024,3]{1,0:T(8,128)S(1)} fusion(f32[3,262144]{0,1:T(8,128)} %copy.79, s32[1024]{0:T(1024)S(1)} %broadcast_clamp_fusion.6), kind=kCustom, calls=%fused_computation.1.clone | custom fusion | bytes 28672 | tf_op jit(solution)/shard_map/jit(_take)/gather | solution.py:22
  173.1 33.2 %gather_fusion.4 = f32[1024,3]{1,0:T(8,128)S(1)} fusion(f32[3,262144]{0,1:T(8,128)} %copy.79, s32[1024]{0:T(1024)S(1)} %broadcast_clamp_fusion.5), kind=kCustom, calls=%fused_computation.2.clone | custom fusion | bytes 28672 | tf_op jit(solution)/shard_map/jit(_take)/gather | solution.py:22
  206.5 33.4 %gather_fusion.5 = f32[1024,3]{1,0:T(8,128)S(1)} fusion(f32[3,262144]{0,1:T(8,128)} %copy.79, s32[1024]{0:T(1024)S(1)} %broadcast_clamp_fusion.4), kind=kCustom, calls=%fused_computation.3.clone | custom fusion | bytes 28672 | tf_op jit(solution)/shard_map/jit(_take)/gather | solution.py:22
  240.1 33.1 %gather_fusion.6 = f32[1024,3]{1,0:T(8,128)S(1)} fusion(f32[3,262144]{0,1:T(8,128)} %copy.79, s32[1024]{0:T(1024)S(1)} %broadcast_clamp_fusion.3), kind=kCustom, calls=%fused_computation.4.clone | custom fusion | bytes 28672 | tf_op jit(solution)/shard_map/jit(_take)/gather | solution.py:22
  273.4 33.7 %gather_fusion.7 = f32[1024,3]{1,0:T(8,128)S(1)} fusion(f32[3,262144]{0,1:T(8,128)} %copy.79, s32[1024]{0:T(1024)S(1)} %broadcast_clamp_fusion.2), kind=kCustom, calls=%fused_computation.5.clone | custom fusion | bytes 28672 | tf_op jit(solution)/shard_map/jit(_take)/gather | solution.py:22
  307.4 33.0 %gather_fusion.8 = f32[1024,3]{1,0:T(8,128)S(1)} fusion(f32[3,262144]{0,1:T(8,128)} %copy.79, s32[1024]{0:T(1024)S(1)} %broadcast_clamp_fusion.1), kind=kCustom, calls=%fused_computation.6.clone | custom fusion | bytes 28672 | tf_op jit(solution)/shard_map/jit(_take)/gather | solution.py:22
  340.7 33.7 %gather_fusion.9 = f32[1024,3]{1,0:T(8,128)S(1)} fusion(f32[3,262144]{0,1:T(8,128)} %copy.79, s32[1024]{0:T(1024)S(1)} %broadcast_clamp_fusion), kind=kCustom, calls=%fused_computation.7.clone | custom fusion | bytes 28672 | tf_op jit(solution)/shard_map/jit(_take)/gather | solution.py:22
  374.6 0.6 broadcast.419
  375.2 0.7 reduce.24
  376.1 0.7 reshape.330
  376.8 18.2 %all-to-all-start.2 = ((f32[16,1,192]{2,1,0:T(1,128)}), f32[16,1,192]{2,1,0:T(1,128)S(1)}, u32[]{:S(2)}, u32[]{:S(2)}) async-start(f32[16,1,192]{2,1,0:T(1,128)} %reshape.330), calls=%async_computation.2 | async-start | bytes 32768 | tf_op jit(solution)/shard_map/all_to_all | solution.py:69
  395.1 6.5 %all-to-all-done.2 = f32[16,1,192]{2,1,0:T(1,128)S(1)} async-done(((f32[16,1,192]{2,1,0:T(1,128)}), f32[16,1,192]{2,1,0:T(1,128)S(1)}, u32[]{:S(2)}, u32[]{:S(2)}) %all-to-all-start.2) | async-done | bytes 12320 | tf_op jit(solution)/shard_map/all_to_all | solution.py:69
  401.6 0.7 reduce.25
  402.6 1.0 gather_fusion.1
  403.7 0.4 fusion.25
  404.1 0.3 convolution_multiply_fusion.6
  404.3 0.3 fusion.5
  404.6 0.3 convolution_bitcast_fusion.2
  404.9 0.3 convolution_multiply_fusion.4
  405.2 0.3 fusion.11
  405.5 0.3 convolution_bitcast_fusion.1
  405.8 0.3 convolution_multiply_fusion.2
  406.0 0.3 fusion.17
  406.3 0.3 convolution_bitcast_fusion
  406.6 0.3 convolution_multiply_fusion
  406.9 1.0 fusion.23
  (60 shorter events, 3.9 us)
Async XLA Ops:
  0.0 34.8 %copy-start = (f32[64,64]{1,0:T(8,128)S(1)}, f32[64,64]{1,0:T(8,128)}, u32[]{:S(2)}) copy-start(f32[64,64]{1,0:T(8,128)} %param.17) | copy-start | bytes 49156
  0.0 404.0 %copy-start.2 = (f32[64,512]{1,0:T(8,128)S(1)}, f32[64,512]{1,0:T(8,128)}, u32[]{:S(2)}) copy-start(f32[64,512]{1,0:T(8,128)} %param.12) | copy-start | bytes 393220
  0.0 95.2 %copy-start.3 = (f32[3,512]{1,0:T(4,128)S(1)}, f32[3,512]{1,0:T(4,128)}, u32[]{:S(2)}) copy-start(f32[3,512]{1,0:T(4,128)} %param.15) | copy-start | bytes 18436
  0.0 404.0 %copy-start.1 = (f32[64,64]{1,0:T(8,128)S(1)}, f32[64,64]{1,0:T(8,128)}, u32[]{:S(2)}) copy-start(f32[64,64]{1,0:T(8,128)} %param.19) | copy-start | bytes 49156
  0.0 404.3 %copy-start.4 = (f32[64,64]{1,0:T(8,128)S(1)}, f32[64,64]{1,0:T(8,128)}, u32[]{:S(2)}) copy-start(f32[64,64]{1,0:T(8,128)} %param.18) | copy-start | bytes 49156
  26.7 71.5 %all-to-all-start.1 = ((s32[16,1,192]{2,1,0:T(1,128)}), s32[16,1,192]{2,1,0:T(1,128)S(1)}, u32[]{:S(2)}, u32[]{:S(2)}) async-start(s32[16,1,192]{2,1,0:T(1,128)} %reshape.326), calls=%async_computation.1 | async-start | bytes 32768 | tf_op jit(solution)/shard_map/all_to_all | solution.py:66
  98.2 276.4 %all-to-all-start = ((f32[16,1,192]{2,1,0:T(1,128)}), f32[16,1,192]{2,1,0:T(1,128)S(1)}, u32[]{:S(2)}, u32[]{:S(2)}) async-start(f32[16,1,192]{2,1,0:T(1,128)} %reshape.328), calls=%async_computation | async-start | bytes 32768 | tf_op jit(solution)/shard_map/all_to_all | solution.py:67
  376.8 24.7 %all-to-all-start.2 = ((f32[16,1,192]{2,1,0:T(1,128)}), f32[16,1,192]{2,1,0:T(1,128)S(1)}, u32[]{:S(2)}, u32[]{:S(2)}) async-start(f32[16,1,192]{2,1,0:T(1,128)} %reshape.330), calls=%async_computation.2 | async-start | bytes 32768 | tf_op jit(solution)/shard_map/all_to_all | solution.py:69
where the time goes:
time: 411 us; the launch traced here: 408 us
  local copies, waits for them, and re-layouts  344 us (84%)
  starting transfers between devices  31.6 us (8%)
  other arithmetic  20.3 us (5%)
  waiting for transfers between devices  6.49 us (2%)
  matrix products  4.86 us (1%)
    gather x16, local copies, waits for them, and re-layouts, corner_sum(): picked = jnp.take(fields, where.astype(jnp.int32), axis=1)  268 us
    unnamed x19, local copies, waits for them, and re-layouts  61.9 us
    all_to_all x1, starting transfers between devices, shards(): lax.all_to_all(values, 'brick', split_axis=1, concat_axis=1, tiled=True)  18.2 us
  transfers between devices with their start and end apart: 3, of which 1 were waited for; matrix products, arithmetic and copies ran while one was open for 82% of the time, Pallas kernels for 0%

commit v1 on v0

v1 whole, which is shorter than its diff:
```python
import functools

import jax
import jax.numpy as jnp
from jax import lax
from jax.experimental import pallas as pl
from jax.experimental.pallas import tpu as pltpu
from jax.sharding import PartitionSpec as P

BS = 64
LANES = 128
HALF = LANES // 2
STEPS = 4
MESH = pl.DeviceIdType.MESH


def iota(shape, dim):
    return lax.broadcasted_iota(jnp.int32, shape, dim)


def pieces(x, count=3):
    out = []
    for _ in range(count):
        high = x.astype(jnp.bfloat16)
        out.append(high)
        x = x - high.astype(jnp.float32)
    return out


def mxu(a, b, contract=((1,), (0,))):
    return lax.dot_general(a, b, (contract, ((), ())), preferred_element_type=jnp.float32)


NT = ((1,), (1,))


def partner(me, d, n):
    return {"brick": lax.rem(me + d, n)}


def greet(me, n):
    barrier = pltpu.get_barrier_semaphore()
    for d in range(1, n):
        pl.semaphore_signal(barrier, inc=1, device_id=partner(me, d, n), device_id_type=MESH)
    return barrier


def request(
    n, owner_ref, coords_ref, fracs_ref, got_ref, index_ref, rank_ref,
    pad, send, recv, send_sem, recv_sem,
):
    me = lax.axis_index("brick")
    barrier = greet(me, n)

    tracers = owner_ref.shape[1]
    rel = owner_ref[...] - me
    rel = jnp.where(rel < 0, rel + n, rel)
    onehot = jnp.where(iota((n, tracers), 0) == rel, 1.0, 0.0)
    upto = jnp.where(iota((LANES, LANES), 0) <= iota((LANES, LANES), 1), 1.0, 0.0)
    upto = upto.astype(jnp.bfloat16)
    running = jnp.zeros((n, 1), jnp.float32)
    ranks = []
    for start in range(0, tracers, LANES):
        part = onehot[:, start : start + LANES]
        counted = mxu(part.astype(jnp.bfloat16), upto) + running
        running = counted[:, LANES - 1 :]
        ranks.append(jnp.sum(part * counted, axis=0, keepdims=True))
    rank = jnp.concatenate(ranks, axis=1).astype(jnp.int32) - 1
    rank_ref[...] = rank
    placed = (iota((LANES, tracers), 0) % HALF) == rank
    placed = jnp.where(placed, 1.0, 0.0).astype(jnp.bfloat16)

    pad[...] = jnp.zeros_like(pad)
    for row in (0, 4):
        pad[0, row : row + 3, :] = coords_ref[...].astype(jnp.float32)
        pad[1, row : row + 3, :] = fracs_ref[...]
    dest = (iota((4 * n, tracers), 0) // 4) == rel
    rows = [pad[0].astype(jnp.bfloat16)] + pieces(pad[1])
    left = []
    for x in rows:
        x = jnp.concatenate([x.astype(jnp.float32)] * (n // 2), axis=0)
        left.append(jnp.where(dest, x, 0.0).astype(jnp.bfloat16))
    packed = mxu(jnp.concatenate(left, axis=0), placed, NT)
    four = 4 * n
    packed = jnp.where(
        iota((four, LANES), 1) < HALF,
        packed[:four],
        packed[four : 2 * four] + packed[2 * four : 3 * four] + packed[3 * four :],
    )
    for d in range(n):
        send[d] = packed[4 * d : 4 * d + 4]
    recv[0] = packed[:4]

    pl.semaphore_wait(barrier, n - 1)
    copies = []
    for d in range(1, n):
        copy = pltpu.make_async_remote_copy(
            src_ref=send.at[d],
            dst_ref=recv.at[d],
            send_sem=send_sem.at[d],
            recv_sem=recv_sem.at[d],
            device_id=partner(me, d, n),
            device_id_type=MESH,
        )
        copy.start()
        copies.append(copy)
    for copy in copies:
        copy.wait()

    low = iota((n, LANES), 1) < HALF
    ci = jnp.where(low, recv[:, 0, :], 0.0).astype(jnp.int32)
    cj = jnp.where(low, recv[:, 1, :], 0.0).astype(jnp.int32)
    base = ci * (BS * BS // LANES)
    index_ref[:n] = base + (cj >> 1)
    index_ref[n:] = base + ((cj + 1) >> 1)
    got_ref[...] = recv[...]


def answer(
    n, cap, index_ref, got_ref, rank_ref, owner_ref, counts_ref, dist_ref, kernel_ref,
    redist_ref, shatter_ref, cells, out_ref,
    w0_ref, w1_ref, stage, rsend, rrecv, rsend_sem, rrecv_sem,
):
    me = lax.axis_index("brick")
    barrier = greet(me, n)

    stage[...] = jnp.zeros_like(stage)
    first, second, third = got_ref[:, 0, :], got_ref[:, 1, :], got_ref[:, 2, :]
    in_low = iota((n, LANES), 1) < HALF
    cj = jnp.where(in_low, second, 0.0).astype(jnp.int32)
    f0 = pltpu.roll(first, HALF, 1)
    f1 = pltpu.roll(second, HALF, 1)
    f2 = pltpu.roll(third, HALF, 1)
    even = jnp.where((cj & 1) == 0, 1.0 - f1, f1)
    columns = jnp.concatenate([third, f2, even, f0], axis=0).T
    lanes = iota((cap, LANES), 1)
    inner = (lanes % HALF).astype(jnp.float32)
    lower = lanes < HALF
    for s in range(n):
        ck = columns[:cap, s : s + 1]
        a2 = columns[:cap, n + s : n + s + 1]
        ae = columns[:cap, 2 * n + s : 2 * n + s + 1]
        a0 = columns[:cap, 3 * n + s : 3 * n + s + 1]
        w = jnp.where(inner == ck, 1.0 - a2, jnp.where(inner == ck + 1.0, a2, 0.0))
        w = w * jnp.where(lower, ae, 1.0 - ae)
        w0_ref[s * cap : (s + 1) * cap, :] = w * (1.0 - a0)
        w1_ref[s * cap : (s + 1) * cap, :] = w * a0

    plane = BS * BS // LANES
    front = iota((3, LANES), 1) < HALF

    def one(s, carry):
        for c in range(cap):
            up = index_ref[s, c]
            dn = index_ref[n + s, c]
            near = jnp.where(front, cells[dn], cells[up])
            far = jnp.where(front, cells[dn + plane], cells[up + plane])
            at = s * cap + c
            acc = near * w0_ref[pl.ds(at, 1), :] + far * w1_ref[pl.ds(at, 1), :]
            stage[pl.ds(s * 4 * HALF + c, 3, stride=HALF), :] = acc
        return carry

    lax.fori_loop(0, n, one, 0)

    ones = jnp.ones((8, LANES), jnp.bfloat16)
    for s in range(n):
        block = stage[s * 4 * HALF : (s + 1) * 4 * HALF, :]
        total = sum(mxu(ones, p, NT) for p in pieces(block))
        rsend[s, 0:1] = total[:1, :LANES]
        rsend[s, 1:2] = total[:1, LANES:]
    rrecv[0] = rsend[0]
    pl.semaphore_wait(barrier, n - 1)
    copies = []
    for d in range(1, n):
        copy = pltpu.make_async_remote_copy(
            src_ref=rsend.at[d],
            dst_ref=rrecv.at[d],
            send_sem=rsend_sem.at[d],
            recv_sem=rrecv_sem.at[d],
            device_id=partner(me, n - d, n),
            device_id_type=MESH,
        )
        copy.start()
        copies.append(copy)

    tracers = owner_ref.shape[1]
    rel = owner_ref[...] - me
    rel = jnp.where(rel < 0, rel + n, rel)
    onehot = jnp.where(iota((n, tracers), 0) == rel, 1.0, 0.0)
    placed = (iota((LANES, tracers), 0) % HALF) == rank_ref[...]
    placed = jnp.where(placed, 1.0, 0.0).astype(jnp.bfloat16)
    for copy in copies:
        copy.wait()

    pair, single = rrecv[:, 0, :], rrecv[:, 1, :]
    spread = jnp.concatenate(
        [
            jnp.where(in_low, pair, 0.0),
            jnp.where(in_low, 0.0, pair),
            jnp.where(in_low, single, 0.0),
        ],
        axis=0,
    )
    found = sum(mxu(p, placed) for p in pieces(spread))
    sampled = [
        jnp.sum(found[f * n : (f + 1) * n] * onehot, axis=0, keepdims=True) for f in range(3)
    ]
    coag = sampled[0] * jnp.sqrt(sampled[1])
    shat = sampled[2] * sampled[1]
    steps = counts_ref[...]
    h = 1.0 / jnp.maximum(steps, 1).astype(jnp.float32)
    dist = dist_ref[...]

    def full(a, b):
        return jnp.dot(a, b, precision=lax.Precision.HIGHEST, preferred_element_type=jnp.float32)

    for section in range(STEPS):
        dot = full(kernel_ref[...], dist)
        gain = coag * full(redist_ref[...], dist * dot)
        gain = gain + shat * full(shatter_ref[...], dist)
        loss = coag * dot + shat
        fresh = (dist + h * gain) / (1.0 + h * loss)
        dist = jnp.where(steps >= section + 1, fresh, dist)
    out_ref[...] = dist


def shards(grid, distribution, owner_ids, coords, fracs, counts, kernel, redist, shatter):
    n = lax.axis_size("brick")
    bins, tracers = distribution.shape
    cap = 2 * tracers // n
    assert cap <= HALF and n % 2 == 0 and tracers % LANES == 0
    vmem = pl.BlockSpec(memory_space=pltpu.VMEM)
    smem = pl.BlockSpec(memory_space=pltpu.SMEM)
    f32 = jnp.float32
    owner = owner_ids.reshape(1, tracers)
    got, index, rank = pl.pallas_call(
        functools.partial(request, n),
        out_shape=(
            jax.ShapeDtypeStruct((n, 4, LANES), f32),
            jax.ShapeDtypeStruct((2 * n, LANES), jnp.int32),
            jax.ShapeDtypeStruct((1, tracers), jnp.int32),
        ),
        in_specs=[vmem] * 3,
        out_specs=(vmem, vmem, vmem),
        scratch_shapes=[
            pltpu.VMEM((2, 8, tracers), f32),
            pltpu.VMEM((n, 4, LANES), f32),
            pltpu.VMEM((n, 4, LANES), f32),
            pltpu.SemaphoreType.DMA((n,)),
            pltpu.SemaphoreType.DMA((n,)),
        ],
        compiler_params=pltpu.CompilerParams(
            collective_id=0, has_side_effects=True, vmem_limit_bytes=8 * 1024 * 1024
        ),
        name="request",
    )(owner, coords, fracs)
    cells = jnp.swapaxes(grid.reshape(grid.shape[0], -1, LANES), 0, 1)
    return pl.pallas_call(
        functools.partial(answer, n, cap),
        out_shape=jax.ShapeDtypeStruct((bins, tracers), f32),
        in_specs=[smem] + [vmem] * 9,
        out_specs=vmem,
        scratch_shapes=[
            pltpu.VMEM((n * cap, LANES), f32),
            pltpu.VMEM((n * cap, LANES), f32),
            pltpu.VMEM((n * 4 * HALF, LANES), f32),
            pltpu.VMEM((n, 2, LANES), f32),
            pltpu.VMEM((n, 2, LANES), f32),
            pltpu.SemaphoreType.DMA((n,)),
            pltpu.SemaphoreType.DMA((n,)),
        ],
        compiler_params=pltpu.CompilerParams(
            collective_id=1, has_side_effects=True, vmem_limit_bytes=24 * 1024 * 1024
        ),
        name="answer",
    )(
        index, got, rank, owner, counts.reshape(1, tracers), distribution, kernel, redist,
        shatter, cells,
    )


def solution(mesh):
    in_specs = (
        P(None, ("runs", "brick")),
        P(None, ("runs", "brick")),
        P(("runs", "brick"), None),
        P(None, ("runs", "brick")),
        P(None, ("runs", "brick")),
        P(("runs", "brick")),
        P(),
        P(),
        P(),
    )
    out_specs = P(None, ("runs", "brick"))
    return jax.shard_map(shards, mesh=mesh, in_specs=in_specs, out_specs=out_specs, check_vma=False)
```

time: 411 us -> 33.7 us (0.08)
  local copies, waits for them, and re-layouts: 344 us -> 9.45 us
  starting transfers between devices: 31.6 us -> 0 us
  Pallas kernels: 0 us -> 23.7 us
  other arithmetic: 20.3 us -> 0 us
  waiting for transfers between devices: 6.49 us -> 0 us
  matrix products: 4.86 us -> 0 us
    gather x19 -> x0, local copies, waits for them, and re-layouts: 274 us -> none  [the longest x16 268 us: corner_sum(): picked = jnp.take(fields, where.astype(jnp.int32), axis=1)]
    unnamed x19 -> x21, local copies, waits for them, and re-layouts: 61.9 us -> 9.45 us
    all_to_all x3 -> x0, starting transfers between devices: 31.6 us -> none  [the longest x1 18.2 us: shards(): lax.all_to_all(values, 'brick', split_axis=1, concat_axis=1, tiled=True)]
    pallas_call x0 -> x2, Pallas kernels: none -> 23.7 us  [the longest x1 15 us: shards(): pl.pallas_call(functools.partial(answer, n, cap), out_shape=jax.ShapeDtyp...]
    all_to_all x3 -> x0, waiting for transfers between devices: 6.49 us -> none  [the longest x1 6.48 us: shards(): lax.all_to_all(values, 'brick', split_axis=1, concat_axis=1, tiled=True)]
    scatter x3 -> x0, local copies, waits for them, and re-layouts: 6.12 us -> none  [the longest x2 3.68 us: packed(): jnp.zeros((lead, bricks * capacity), values.dtype).at[:, slot].set(values)]
    sub x2 -> x0, other arithmetic: 5.5 us -> none  [the longest x1 5.49 us: slot_of(): ranked = jnp.arange(owner.shape[0], dtype=jnp.int32) - starts[owner[order]]]
    dot_general x12 -> x0, matrix products: 4.86 us -> none  [the longest x4 1.95 us: advance(): jnp.einsum('ij,j...->i...', kernel, dist, precision=lax.Precision.HIGHEST)]
  transfers between devices with their start and end apart: 3 -> 0, of which waited for: 1 -> 0; matrix products, arithmetic and copies ran while one was open for 82% -> 0% of each run, Pallas kernels for 0% -> 0%
where the time goes in v1:
time: 33.7 us; the launch traced here: 33.2 us
  Pallas kernels  23.7 us (70%)
  local copies, waits for them, and re-layouts  9.45 us (28%)
    pallas_call x1, Pallas kernels, shards(): pl.pallas_call(functools.partial(answer, n, cap), out_shape=jax.ShapeDtyp...  15 us
    unnamed x21, local copies, waits for them, and re-layouts  9.45 us
    pallas_call x1, Pallas kernels, shards(): pl.pallas_call(functools.partial(request, n), out_shape=(jax.ShapeDtypeSt...  8.67 us

profile of v1, /device:TPU:0, one launch (start us, length us, event | category | flops | bytes accessed | tf_op | source)
XLA Modules:
  0.0 33.2 jit_solution(1332238854089992151)
XLA Ops:
  0.0 0.0 copy-start.5
  0.0 0.7 %copy-done.5 = s32[512,1]{0,1:T(1,128)S(1)} copy-done((s32[512,1]{0,1:T(1,128)S(1)}, s32[512,1]{0,1:T(1,128)}, u32[]{:S(2)}) %copy-start.5) | copy-done | bytes 2072
  0.7 0.0 copy-start.7
  0.7 0.7 %copy-done.7 = s32[3,512]{1,0:T(4,128)S(1)} copy-done((s32[3,512]{1,0:T(4,128)S(1)}, s32[3,512]{1,0:T(4,128)}, u32[]{:S(2)}) %copy-start.7) | copy-done | bytes 6168
  1.4 0.0 copy-start.8
  1.4 0.7 %copy-done.8 = f32[3,512]{1,0:T(4,128)S(1)} copy-done((f32[3,512]{1,0:T(4,128)S(1)}, f32[3,512]{1,0:T(4,128)}, u32[]{:S(2)}) %copy-start.8) | copy-done | bytes 6168
  2.1 8.7 %request.1 = (f32[16,4,128]{2,1,0:T(4,128)S(1)}, s32[32,128]{1,0:T(8,128)S(1)}, s32[1,512]{1,0:T(1,128)S(1)}) custom-call(s32[1,512]{1,0:T(1,128)S(1)} %bitcast.6, s32[3,512]{1,0:T(4,128)S(1)} %copy-done.7, f32[3,512]{1,0:T(4,128)S(1)} %copy-done.8), custom_call_target="tpu_custom_call" | custom-call | tf_op jit(solution)/shard_map/request/pallas_call | solution.py:236
  10.8 0.0 copy-start
  10.8 2.2 %copy-done = f32[3,262144]{1,0:T(4,128)S(1)} copy-done((f32[3,262144]{1,0:T(4,128)S(1)}, f32[3,262144]{1,0:T(4,128)}, u32[]{:S(2)}) %copy-start) | copy-done | bytes 3145752
  12.9 0.0 copy-start.1
  12.9 0.9 %copy-done.1 = f32[64,512]{1,0:T(8,128)S(1)} copy-done((f32[64,512]{1,0:T(8,128)S(1)}, f32[64,512]{1,0:T(8,128)}, u32[]{:S(2)}) %copy-start.1) | copy-done | bytes 131096
  13.8 0.0 copy-start.2
  13.8 0.8 %copy-done.2 = f32[64,64]{1,0:T(8,128)S(1)} copy-done((f32[64,64]{1,0:T(8,128)S(1)}, f32[64,64]{1,0:T(8,128)}, u32[]{:S(2)}) %copy-start.2) | copy-done | bytes 16408
  14.6 0.0 copy-start.3
  14.6 0.8 %copy-done.3 = f32[64,64]{1,0:T(8,128)S(1)} copy-done((f32[64,64]{1,0:T(8,128)S(1)}, f32[64,64]{1,0:T(8,128)}, u32[]{:S(2)}) %copy-start.3) | copy-done | bytes 16408
  15.4 0.0 copy-start.4
  15.4 0.8 %copy-done.4 = f32[64,64]{1,0:T(8,128)S(1)} copy-done((f32[64,64]{1,0:T(8,128)S(1)}, f32[64,64]{1,0:T(8,128)}, u32[]{:S(2)}) %copy-start.4) | copy-done | bytes 16408
  16.1 0.0 copy-start.6
  16.1 0.7 %copy-done.6 = s32[512,1]{0,1:T(1,128)S(1)} copy-done((s32[512,1]{0,1:T(1,128)S(1)}, s32[512,1]{0,1:T(1,128)}, u32[]{:S(2)}) %copy-start.6) | copy-done | bytes 2072
  16.8 0.0 copy-start.9
  16.8 0.7 %copy-done.9 = s32[512]{0:T(512)S(1)} copy-done((s32[512]{0:T(512)S(1)}, s32[512]{0:T(512)}, u32[]{:S(2)}) %copy-start.9) | copy-done | bytes 2072
  17.5 15.0 %answer.1 = f32[64,512]{1,0:T(8,128)S(1)} custom-call(s32[32,128]{1,0:T(8,128)S(1)} %get-tuple-element.8.index_ref, f32[16,4,128]{2,1,0:T(4,128)S(1)} %get-tuple-element.9.got_ref, s32[1,512]{1,0:T(1,128)S(1)} %get-tuple-element.10.rank_ref, s32[1,512]{1,0:T(1,128)S(1)} %bitcast.7, s32[1,512]{1,0:T(1,128)S(1)} %bitcast.8, f32[64,512]{1,0:T(8,128)S(1)} %copy-done.1, ...), custom_call_target="tpu_custom_call" | custom-call | tf_op jit(solution)/shard_map/answer/pallas_call | solution.py:258
  32.5 0.7 %copy.11 = f32[64,512]{1,0:T(8,128)} copy(f32[64,512]{1,0:T(8,128)S(1)} %answer.1) | data formatting | bytes 262144
Async XLA Ops:
  0.0 0.7 %copy-start.5 = (s32[512,1]{0,1:T(1,128)S(1)}, s32[512,1]{0,1:T(1,128)}, u32[]{:S(2)}) copy-start(s32[512,1]{0,1:T(1,128)} %param.11) | copy-start | bytes 6148
  0.7 0.7 %copy-start.7 = (s32[3,512]{1,0:T(4,128)S(1)}, s32[3,512]{1,0:T(4,128)}, u32[]{:S(2)}) copy-start(s32[3,512]{1,0:T(4,128)} %coords_ref.1) | copy-start | bytes 18436
  1.4 0.7 %copy-start.8 = (f32[3,512]{1,0:T(4,128)S(1)}, f32[3,512]{1,0:T(4,128)}, u32[]{:S(2)}) copy-start(f32[3,512]{1,0:T(4,128)} %fracs_ref.1) | copy-start | bytes 18436
  10.8 2.2 %copy-start = (f32[3,262144]{1,0:T(4,128)S(1)}, f32[3,262144]{1,0:T(4,128)}, u32[]{:S(2)}) copy-start(f32[3,262144]{1,0:T(4,128)} %param.9) | copy-start | bytes 9437188
  12.9 0.9 %copy-start.1 = (f32[64,512]{1,0:T(8,128)S(1)}, f32[64,512]{1,0:T(8,128)}, u32[]{:S(2)}) copy-start(f32[64,512]{1,0:T(8,128)} %dist_ref.1) | copy-start | bytes 393220
  13.8 0.8 %copy-start.2 = (f32[64,64]{1,0:T(8,128)S(1)}, f32[64,64]{1,0:T(8,128)}, u32[]{:S(2)}) copy-start(f32[64,64]{1,0:T(8,128)} %kernel_ref.1) | copy-start | bytes 49156
  14.6 0.8 %copy-start.3 = (f32[64,64]{1,0:T(8,128)S(1)}, f32[64,64]{1,0:T(8,128)}, u32[]{:S(2)}) copy-start(f32[64,64]{1,0:T(8,128)} %redist_ref.1) | copy-start | bytes 49156
  15.4 0.8 %copy-start.4 = (f32[64,64]{1,0:T(8,128)S(1)}, f32[64,64]{1,0:T(8,128)}, u32[]{:S(2)}) copy-start(f32[64,64]{1,0:T(8,128)} %shatter_ref.1) | copy-start | bytes 49156
  16.1 0.7 %copy-start.6 = (s32[512,1]{0,1:T(1,128)S(1)}, s32[512,1]{0,1:T(1,128)}, u32[]{:S(2)}) copy-start(s32[512,1]{0,1:T(1,128)} %param.11) | copy-start | bytes 6148
  16.8 0.7 %copy-start.9 = (s32[512]{0:T(512)S(1)}, s32[512]{0:T(512)}, u32[]{:S(2)}) copy-start(s32[512]{0:T(512)} %param.14) | copy-start | bytes 6148

commit v2 on v1

--- a/solution.py
+++ b/solution.py
@@ -11,6 +11,8 @@
 LANES = 128
 HALF = LANES // 2
 STEPS = 4
+KEPT = 6
+GROUPS = 4
 MESH = pl.DeviceIdType.MESH
 
 
@@ -34,6 +36,16 @@
 NT = ((1,), (1,))
 
 
+def wide(x):
+    high, low = pieces(x, 2)
+    return jnp.concatenate([high, high, low], axis=1)
+
+
+def tall(x):
+    high, low = pieces(x, 2)
+    return jnp.concatenate([high, low, high], axis=0)
+
+
 def partner(me, d, n):
     return {"brick": lax.rem(me + d, n)}
 
@@ -46,11 +58,22 @@
 
 
 def request(
-    n, owner_ref, coords_ref, fracs_ref, got_ref, index_ref, rank_ref,
-    pad, send, recv, send_sem, recv_sem,
+    n, owner_hbm, coords_hbm, fracs_hbm, *refs,
 ):
+    kept_hbm, (got_ref, index_ref, rank_ref, owner_ref) = refs[:KEPT], refs[KEPT : KEPT + 4]
+    kept_refs = refs[KEPT + 4 : 2 * KEPT + 4]
+    coords_ref, fracs_ref, pad, send, recv, load_sem, send_sem, recv_sem = refs[2 * KEPT + 4 :]
     me = lax.axis_index("brick")
+    sources = (owner_hbm, coords_hbm, fracs_hbm) + kept_hbm
+    targets = (owner_ref, coords_ref, fracs_ref) + kept_refs
+    loads = [
+        pltpu.make_async_copy(a, b, load_sem.at[i]) for i, (a, b) in enumerate(zip(sources, targets))
+    ]
+    for load in loads:
+        load.start()
     barrier = greet(me, n)
+    for load in loads[:3]:
+        load.wait()
 
     tracers = owner_ref.shape[1]
     rel = owner_ref[...] - me
@@ -114,17 +137,18 @@
     index_ref[:n] = base + (cj >> 1)
     index_ref[n:] = base + ((cj + 1) >> 1)
     got_ref[...] = recv[...]
+    for load in loads[3:]:
+        load.wait()
 
 
 def answer(
-    n, cap, index_ref, got_ref, rank_ref, owner_ref, counts_ref, dist_ref, kernel_ref,
-    redist_ref, shatter_ref, cells, out_ref,
+    n, cap, index_ref, got_ref, rank_ref, owner_ref, cells, counts_ref, dist_ref, kernel_ref,
+    redist_ref, shatter_ref, out_ref,
     w0_ref, w1_ref, stage, rsend, rrecv, rsend_sem, rrecv_sem,
 ):
     me = lax.axis_index("brick")
     barrier = greet(me, n)
 
-    stage[...] = jnp.zeros_like(stage)
     first, second, third = got_ref[:, 0, :], got_ref[:, 1, :], got_ref[:, 2, :]
     in_low = iota((n, LANES), 1) < HALF
     cj = jnp.where(in_low, second, 0.0).astype(jnp.int32)
@@ -157,31 +181,34 @@
             far = jnp.where(front, cells[dn + plane], cells[up + plane])
             at = s * cap + c
             acc = near * w0_ref[pl.ds(at, 1), :] + far * w1_ref[pl.ds(at, 1), :]
-            stage[pl.ds(s * 4 * HALF + c, 3, stride=HALF), :] = acc
+            stage[pl.ds(s * 3 * HALF + c, 3, stride=HALF), :] = acc
         return carry
 
-    lax.fori_loop(0, n, one, 0)
-
     ones = jnp.ones((8, LANES), jnp.bfloat16)
-    for s in range(n):
-        block = stage[s * 4 * HALF : (s + 1) * 4 * HALF, :]
-        total = sum(mxu(ones, p, NT) for p in pieces(block))
-        rsend[s, 0:1] = total[:1, :LANES]
-        rsend[s, 1:2] = total[:1, LANES:]
-    rrecv[0] = rsend[0]
-    pl.semaphore_wait(barrier, n - 1)
+    blank = jnp.zeros((1, HALF), jnp.float32)
+    size = n // GROUPS
     copies = []
-    for d in range(1, n):
-        copy = pltpu.make_async_remote_copy(
-            src_ref=rsend.at[d],
-            dst_ref=rrecv.at[d],
-            send_sem=rsend_sem.at[d],
-            recv_sem=rrecv_sem.at[d],
-            device_id=partner(me, n - d, n),
-            device_id_type=MESH,
-        )
-        copy.start()
-        copies.append(copy)
+    for g in range(GROUPS):
+        lax.fori_loop(g * size, (g + 1) * size, one, 0)
+        for s in range(g * size, (g + 1) * size):
+            block = stage[s * 3 * HALF : (s + 1) * 3 * HALF, :]
+            total = sum(mxu(ones, p, NT) for p in pieces(block))[:1]
+            rsend[s, 0:1] = total[:, :LANES]
+            rsend[s, 1:2] = jnp.concatenate([total[:, LANES:], blank], axis=1)
+        if g == 0:
+            pl.semaphore_wait(barrier, n - 1)
+            rrecv[0] = rsend[0]
+        for d in range(max(1, g * size), (g + 1) * size):
+            copy = pltpu.make_async_remote_copy(
+                src_ref=rsend.at[d],
+                dst_ref=rrecv.at[d],
+                send_sem=rsend_sem.at[d],
+                recv_sem=rrecv_sem.at[d],
+                device_id=partner(me, n - d, n),
+                device_id_type=MESH,
+            )
+            copy.start()
+            copies.append(copy)
 
     tracers = owner_ref.shape[1]
     rel = owner_ref[...] - me
@@ -189,6 +216,19 @@
     onehot = jnp.where(iota((n, tracers), 0) == rel, 1.0, 0.0)
     placed = (iota((LANES, tracers), 0) % HALF) == rank_ref[...]
     placed = jnp.where(placed, 1.0, 0.0).astype(jnp.bfloat16)
+    steps = counts_ref[...]
+    h = 1.0 / jnp.maximum(steps, 1).astype(jnp.float32)
+    dist = dist_ref[...]
+    bins = dist.shape[0]
+    both = wide(jnp.concatenate([kernel_ref[...], shatter_ref[...]], axis=0))
+    moved = wide(redist_ref[...])
+
+    def products(dist):
+        out = mxu(both, tall(dist))
+        dot, broken = out[:bins], out[bins:]
+        return dot, broken, mxu(moved, tall(dist * dot))
+
+    ready = products(dist)
     for copy in copies:
         copy.wait()
 
@@ -207,17 +247,9 @@
     ]
     coag = sampled[0] * jnp.sqrt(sampled[1])
     shat = sampled[2] * sampled[1]
-    steps = counts_ref[...]
-    h = 1.0 / jnp.maximum(steps, 1).astype(jnp.float32)
-    dist = dist_ref[...]
-
-    def full(a, b):
-        return jnp.dot(a, b, precision=lax.Precision.HIGHEST, preferred_element_type=jnp.float32)
-
     for section in range(STEPS):
-        dot = full(kernel_ref[...], dist)
-        gain = coag * full(redist_ref[...], dist * dot)
-        gain = gain + shat * full(shatter_ref[...], dist)
+        dot, broken, back = ready if section == 0 else products(dist)
+        gain = coag * back + shat * broken
         loss = coag * dot + shat
         fresh = (dist + h * gain) / (1.0 + h * loss)
         dist = jnp.where(steps >= section + 1, fresh, dist)
@@ -232,38 +264,47 @@
     vmem = pl.BlockSpec(memory_space=pltpu.VMEM)
     smem = pl.BlockSpec(memory_space=pltpu.SMEM)
     f32 = jnp.float32
-    owner = owner_ids.reshape(1, tracers)
-    got, index, rank = pl.pallas_call(
+    hbm = pl.BlockSpec(memory_space=pltpu.HBM)
+    kept = (
+        jnp.swapaxes(grid.reshape(grid.shape[0], -1, LANES), 0, 1),
+        counts.reshape(1, tracers), distribution, kernel, redist, shatter,
+    )
+    assert len(kept) == KEPT
+    got, index, rank, owner, *kept = pl.pallas_call(
         functools.partial(request, n),
         out_shape=(
             jax.ShapeDtypeStruct((n, 4, LANES), f32),
             jax.ShapeDtypeStruct((2 * n, LANES), jnp.int32),
             jax.ShapeDtypeStruct((1, tracers), jnp.int32),
+            jax.ShapeDtypeStruct((1, tracers), jnp.int32),
+            *[jax.ShapeDtypeStruct(x.shape, x.dtype) for x in kept],
         ),
-        in_specs=[vmem] * 3,
-        out_specs=(vmem, vmem, vmem),
+        in_specs=[hbm] * (3 + KEPT),
+        out_specs=(vmem,) * (4 + KEPT),
         scratch_shapes=[
+            pltpu.VMEM(coords.shape, jnp.int32),
+            pltpu.VMEM(fracs.shape, f32),
             pltpu.VMEM((2, 8, tracers), f32),
             pltpu.VMEM((n, 4, LANES), f32),
             pltpu.VMEM((n, 4, LANES), f32),
+            pltpu.SemaphoreType.DMA((3 + KEPT,)),
             pltpu.SemaphoreType.DMA((n,)),
             pltpu.SemaphoreType.DMA((n,)),
         ],
         compiler_params=pltpu.CompilerParams(
-            collective_id=0, has_side_effects=True, vmem_limit_bytes=8 * 1024 * 1024
+            collective_id=0, has_side_effects=True, vmem_limit_bytes=16 * 1024 * 1024
         ),
         name="request",
-    )(owner, coords, fracs)
-    cells = jnp.swapaxes(grid.reshape(grid.shape[0], -1, LANES), 0, 1)
+    )(*[pltpu.with_memory_space_constraint(x, pltpu.HBM) for x in (owner_ids.reshape(1, tracers), coords, fracs, *kept)])
     return pl.pallas_call(
         functools.partial(answer, n, cap),
         out_shape=jax.ShapeDtypeStruct((bins, tracers), f32),
-        in_specs=[smem] + [vmem] * 9,
+        in_specs=[smem] + [vmem] * (3 + KEPT),
         out_specs=vmem,
         scratch_shapes=[
             pltpu.VMEM((n * cap, LANES), f32),
             pltpu.VMEM((n * cap, LANES), f32),
-            pltpu.VMEM((n * 4 * HALF, LANES), f32),
+            pltpu.VMEM((n * 3 * HALF, LANES), f32),
             pltpu.VMEM((n, 2, LANES), f32),
             pltpu.VMEM((n, 2, LANES), f32),
             pltpu.SemaphoreType.DMA((n,)),
@@ -273,10 +314,7 @@
             collective_id=1, has_side_effects=True, vmem_limit_bytes=24 * 1024 * 1024
         ),
         name="answer",
-    )(
-        index, got, rank, owner, counts.reshape(1, tracers), distribution, kernel, redist,
-        shatter, cells,
-    )
+    )(index, got, rank, owner, *kept)
 
 
 def solution(mesh):

time: 33.7 us -> 24 us (0.71); the launches traced: 33.2 us -> 23.9 us
  local copies, waits for them, and re-layouts: 9.45 us -> 0.66 us
  Pallas kernels: 23.7 us -> 23.2 us
    unnamed x21 -> x1, local copies, waits for them, and re-layouts: 9.45 us -> 0.66 us
    pallas_call x1, Pallas kernels: 15 us -> 13.9 us  [shards(): pl.pallas_call(functools.partial(answer, n, cap), out_shape=jax.ShapeDtyp...]
    pallas_call x1, Pallas kernels: 8.67 us -> 9.34 us  [shards(): pl.pallas_call(functools.partial(request, n), out_shape=(jax.ShapeDtypeSt...]
where the time goes in v2:
time: 24 us; the launch traced here: 23.9 us
  Pallas kernels  23.2 us (97%)
  local copies, waits for them, and re-layouts  0.66 us (3%)
    pallas_call x1, Pallas kernels, shards(): pl.pallas_call(functools.partial(answer, n, cap), out_shape=jax.ShapeDtyp...  13.9 us
    pallas_call x1, Pallas kernels, shards(): pl.pallas_call(functools.partial(request, n), out_shape=(jax.ShapeDtypeSt...  9.34 us
    unnamed x1, local copies, waits for them, and re-layouts  0.66 us

profile of v2, /device:TPU:0, one launch (start us, length us, event | category | flops | bytes accessed | tf_op | source)
XLA Modules:
  0.0 23.9 jit_solution(7985722772045743244)
XLA Ops:
  0.0 9.3 %request.1 = (f32[16,4,128]{2,1,0:T(4,128)S(1)}, s32[32,128]{1,0:T(8,128)S(1)}, s32[1,512]{1,0:T(1,128)S(1)}, s32[1,512]{1,0:T(1,128)S(1)}, f32[2048,3,128]{2,1,...) custom-call(s32[1,512]{1,0:T(1,128)} %bitcast.6, ...), custom_call_target="tpu_custom_call" | custom-call | tf_op jit(solution)/shard_map/request/pallas_call | solution.py:273
  9.3 13.9 %answer.1 = f32[64,512]{1,0:T(8,128)S(1)} custom-call(s32[32,128]{1,0:T(8,128)S(1)} %get-tuple-element.15.index_ref, f32[16,4,128]{2,1,0:T(4,128)S(1)} %get-tuple-element.16.got_ref, s32[1,512]{1,0:T(1,128)S(1)} %get-tuple-element.17.rank_ref, s32[1,512]{1,0:T(1,128)S(1)} %get-tuple-element.18.owner_ref, f32[2048,3,128]{2,1,0:T(4,128)S(1)} %get-tuple-element.19.cells, ...), custom_call_target="tpu_custom_call" | custom-call | tf_op jit(solution)/shard_map/answer/pallas_call | solution.py:299
  23.2 0.7 %copy.11 = f32[64,512]{1,0:T(8,128)} copy(f32[64,512]{1,0:T(8,128)S(1)} %answer.1) | data formatting | bytes 262144

commit v3 on v2

--- a/solution.py
+++ b/solution.py
@@ -12,7 +12,6 @@
 HALF = LANES // 2
 STEPS = 4
 KEPT = 6
-GROUPS = 4
 MESH = pl.DeviceIdType.MESH
 
 
@@ -144,71 +143,86 @@
 def answer(
     n, cap, index_ref, got_ref, rank_ref, owner_ref, cells, counts_ref, dist_ref, kernel_ref,
     redist_ref, shatter_ref, out_ref,
-    w0_ref, w1_ref, stage, rsend, rrecv, rsend_sem, rrecv_sem,
+    index_s, wa0, wa1, wb0, wb1, stage_a, stage_b, rsend, rrecv, index_sem, rsend_sem, rrecv_sem,
 ):
     me = lax.axis_index("brick")
+    index_copy = pltpu.make_async_copy(index_ref, index_s, index_sem)
+    index_copy.start()
     barrier = greet(me, n)
-
-    first, second, third = got_ref[:, 0, :], got_ref[:, 1, :], got_ref[:, 2, :]
     in_low = iota((n, LANES), 1) < HALF
-    cj = jnp.where(in_low, second, 0.0).astype(jnp.int32)
-    f0 = pltpu.roll(first, HALF, 1)
-    f1 = pltpu.roll(second, HALF, 1)
-    f2 = pltpu.roll(third, HALF, 1)
-    even = jnp.where((cj & 1) == 0, 1.0 - f1, f1)
-    columns = jnp.concatenate([third, f2, even, f0], axis=0).T
     lanes = iota((cap, LANES), 1)
     inner = (lanes % HALF).astype(jnp.float32)
     lower = lanes < HALF
-    for s in range(n):
-        ck = columns[:cap, s : s + 1]
-        a2 = columns[:cap, n + s : n + s + 1]
-        ae = columns[:cap, 2 * n + s : 2 * n + s + 1]
-        a0 = columns[:cap, 3 * n + s : 3 * n + s + 1]
+    plane = BS * BS // LANES
+    front = iota((3, LANES), 1) < HALF
+    ones = jnp.ones((8, 2 * LANES), jnp.bfloat16)
+    blank = jnp.zeros((1, HALF), jnp.float32)
+
+    def weigh(d, w0_ref, w1_ref):
+        block = got_ref[d]
+        turned = pltpu.roll(block, HALF, 1)
+        odd = (block.astype(jnp.int32) & 1) == 1
+        even = jnp.where(odd, turned, 1.0 - turned)
+        columns = jnp.concatenate([block, even], axis=0).T
+        ck = columns[:cap, 2:3]
+        ae = columns[:cap, 5:6]
+        a0 = columns[HALF : HALF + cap, 0:1]
+        a2 = columns[HALF : HALF + cap, 2:3]
         w = jnp.where(inner == ck, 1.0 - a2, jnp.where(inner == ck + 1.0, a2, 0.0))
         w = w * jnp.where(lower, ae, 1.0 - ae)
-        w0_ref[s * cap : (s + 1) * cap, :] = w * (1.0 - a0)
-        w1_ref[s * cap : (s + 1) * cap, :] = w * a0
-
-    plane = BS * BS // LANES
-    front = iota((3, LANES), 1) < HALF
-
-    def one(s, carry):
+        w0_ref[...] = w * (1.0 - a0)
+        w1_ref[...] = w * a0
+
+    def gather(d, w0_ref, w1_ref, stage):
         for c in range(cap):
-            up = index_ref[s, c]
-            dn = index_ref[n + s, c]
+            up = index_s[d, c]
+            dn = index_s[n + d, c]
             near = jnp.where(front, cells[dn], cells[up])
             far = jnp.where(front, cells[dn + plane], cells[up + plane])
-            at = s * cap + c
-            acc = near * w0_ref[pl.ds(at, 1), :] + far * w1_ref[pl.ds(at, 1), :]
-            stage[pl.ds(s * 3 * HALF + c, 3, stride=HALF), :] = acc
+            acc = near * w0_ref[c : c + 1, :] + far * w1_ref[c : c + 1, :]
+            stage[pl.ds(c, 3, stride=HALF), :] = acc
+
+    def reduce(stage):
+        total = mxu(ones, jnp.concatenate(pieces(stage[...], 2), axis=1), NT)[:1]
+        return total[:, :LANES], jnp.concatenate([total[:, LANES:], blank], axis=1)
+
+    def back(d):
+        return pltpu.make_async_remote_copy(
+            src_ref=rsend.at[d],
+            dst_ref=rrecv.at[d],
+            send_sem=rsend_sem.at[d],
+            recv_sem=rrecv_sem.at[d],
+            device_id=partner(me, n - d, n),
+            device_id_type=MESH,
+        )
+
+    def finish(d, stage):
+        rsend[d, 0:1], rsend[d, 1:2] = reduce(stage)
+        back(d).start()
+
+    if cap < HALF:
+        stage_a[...] = jnp.zeros_like(stage_a)
+        stage_b[...] = jnp.zeros_like(stage_b)
+    weigh(1, wa0, wa1)
+    index_copy.wait()
+    gather(1, wa0, wa1, stage_a)
+    weigh(2, wb0, wb1)
+    pl.semaphore_wait(barrier, n - 1)
+
+    def two(i, carry):
+        d = 2 * i + 2
+        weigh(d + 1, wa0, wa1)
+        gather(d, wb0, wb1, stage_b)
+        finish(d - 1, stage_a)
+        weigh(lax.rem(d + 2, n), wb0, wb1)
+        gather(d + 1, wa0, wa1, stage_a)
+        finish(d, stage_b)
         return carry
 
-    ones = jnp.ones((8, LANES), jnp.bfloat16)
-    blank = jnp.zeros((1, HALF), jnp.float32)
-    size = n // GROUPS
-    copies = []
-    for g in range(GROUPS):
-        lax.fori_loop(g * size, (g + 1) * size, one, 0)
-        for s in range(g * size, (g + 1) * size):
-            block = stage[s * 3 * HALF : (s + 1) * 3 * HALF, :]
-            total = sum(mxu(ones, p, NT) for p in pieces(block))[:1]
-            rsend[s, 0:1] = total[:, :LANES]
-            rsend[s, 1:2] = jnp.concatenate([total[:, LANES:], blank], axis=1)
-        if g == 0:
-            pl.semaphore_wait(barrier, n - 1)
-            rrecv[0] = rsend[0]
-        for d in range(max(1, g * size), (g + 1) * size):
-            copy = pltpu.make_async_remote_copy(
-                src_ref=rsend.at[d],
-                dst_ref=rrecv.at[d],
-                send_sem=rsend_sem.at[d],
-                recv_sem=rrecv_sem.at[d],
-                device_id=partner(me, n - d, n),
-                device_id_type=MESH,
-            )
-            copy.start()
-            copies.append(copy)
+    lax.fori_loop(0, n // 2 - 1, two, 0)
+    gather(0, wb0, wb1, stage_b)
+    finish(n - 1, stage_a)
+    rrecv[0, 0:1], rrecv[0, 1:2] = reduce(stage_b)
 
     tracers = owner_ref.shape[1]
     rel = owner_ref[...] - me
@@ -229,8 +243,8 @@
         return dot, broken, mxu(moved, tall(dist * dot))
 
     ready = products(dist)
-    for copy in copies:
-        copy.wait()
+    for d in range(1, n):
+        back(d).wait()
 
     pair, single = rrecv[:, 0, :], rrecv[:, 1, :]
     spread = jnp.concatenate(
@@ -248,8 +262,8 @@
     coag = sampled[0] * jnp.sqrt(sampled[1])
     shat = sampled[2] * sampled[1]
     for section in range(STEPS):
-        dot, broken, back = ready if section == 0 else products(dist)
-        gain = coag * back + shat * broken
+        dot, broken, spilt = ready if section == 0 else products(dist)
+        gain = coag * spilt + shat * broken
         loss = coag * dot + shat
         fresh = (dist + h * gain) / (1.0 + h * loss)
         dist = jnp.where(steps >= section + 1, fresh, dist)
@@ -262,7 +276,6 @@
     cap = 2 * tracers // n
     assert cap <= HALF and n % 2 == 0 and tracers % LANES == 0
     vmem = pl.BlockSpec(memory_space=pltpu.VMEM)
-    smem = pl.BlockSpec(memory_space=pltpu.SMEM)
     f32 = jnp.float32
     hbm = pl.BlockSpec(memory_space=pltpu.HBM)
     kept = (
@@ -299,14 +312,15 @@
     return pl.pallas_call(
         functools.partial(answer, n, cap),
         out_shape=jax.ShapeDtypeStruct((bins, tracers), f32),
-        in_specs=[smem] + [vmem] * (3 + KEPT),
+        in_specs=[vmem] * (4 + KEPT),
         out_specs=vmem,
         scratch_shapes=[
-            pltpu.VMEM((n * cap, LANES), f32),
-            pltpu.VMEM((n * cap, LANES), f32),
-            pltpu.VMEM((n * 3 * HALF, LANES), f32),
+            pltpu.SMEM((2 * n, LANES), jnp.int32),
+            *[pltpu.VMEM((cap, LANES), f32)] * 4,
+            *[pltpu.VMEM((3 * HALF, LANES), f32)] * 2,
             pltpu.VMEM((n, 2, LANES), f32),
             pltpu.VMEM((n, 2, LANES), f32),
+            pltpu.SemaphoreType.DMA,
             pltpu.SemaphoreType.DMA((n,)),
             pltpu.SemaphoreType.DMA((n,)),
         ],

time: 24 us -> 25 us (1.042)
  Pallas kernels: 23.2 us -> 24.2 us
    pallas_call x1, Pallas kernels: 13.9 us -> 14.8 us  [shards(): pl.pallas_call(functools.partial(answer, n, cap), out_shape=jax.ShapeDtyp...]
where the time goes in v3:
time: 25 us; the launch traced here: 24.8 us
  Pallas kernels  24.2 us (97%)
  local copies, waits for them, and re-layouts  0.66 us (3%)
    pallas_call x1, Pallas kernels, shards(): pl.pallas_call(functools.partial(answer, n, cap), out_shape=jax.ShapeDtyp...  14.8 us
    pallas_call x1, Pallas kernels, shards(): pl.pallas_call(functools.partial(request, n), out_shape=(jax.ShapeDtypeSt...  9.34 us
    unnamed x1, local copies, waits for them, and re-layouts  0.66 us

profile of v3, /device:TPU:0, one launch (start us, length us, event | category | flops | bytes accessed | tf_op | source)
XLA Modules:
  0.0 24.8 jit_solution(13806218025158606645)
XLA Ops:
  0.0 9.3 %request.1 = (f32[16,4,128]{2,1,0:T(4,128)S(1)}, s32[32,128]{1,0:T(8,128)S(1)}, s32[1,512]{1,0:T(1,128)S(1)}, s32[1,512]{1,0:T(1,128)S(1)}, f32[2048,3,128]{2,1,...) custom-call(s32[1,512]{1,0:T(1,128)} %bitcast.6, ...), custom_call_target="tpu_custom_call" | custom-call | tf_op jit(solution)/shard_map/request/pallas_call | solution.py:286
  9.3 14.8 %answer.1 = f32[64,512]{1,0:T(8,128)S(1)} custom-call(s32[32,128]{1,0:T(8,128)S(1)} %get-tuple-element.15.index_ref, f32[16,4,128]{2,1,0:T(4,128)S(1)} %get-tuple-element.16.got_ref, s32[1,512]{1,0:T(1,128)S(1)} %get-tuple-element.17.rank_ref, s32[1,512]{1,0:T(1,128)S(1)} %get-tuple-element.18.owner_ref, f32[2048,3,128]{2,1,0:T(4,128)S(1)} %get-tuple-element.19.cells, ...), custom_call_target="tpu_custom_call" | custom-call | tf_op jit(solution)/shard_map/answer/pallas_call | solution.py:312
  24.2 0.7 %copy.11 = f32[64,512]{1,0:T(8,128)} copy(f32[64,512]{1,0:T(8,128)S(1)} %answer.1) | data formatting | bytes 262144

commit v4 on v3

--- a/solution.py
+++ b/solution.py
@@ -12,6 +12,7 @@
 HALF = LANES // 2
 STEPS = 4
 KEPT = 6
+CHUNK = 32
 MESH = pl.DeviceIdType.MESH
 
 
@@ -57,14 +58,17 @@
 
 
 def request(
-    n, owner_hbm, coords_hbm, fracs_hbm, *refs,
+    n, cap, owner_hbm, coords_hbm, fracs_hbm, *refs,
 ):
-    kept_hbm, (got_ref, index_ref, rank_ref, owner_ref) = refs[:KEPT], refs[KEPT : KEPT + 4]
-    kept_refs = refs[KEPT + 4 : 2 * KEPT + 4]
-    coords_ref, fracs_ref, pad, send, recv, load_sem, send_sem, recv_sem = refs[2 * KEPT + 4 :]
+    kept_hbm = refs[:KEPT]
+    w0_ref, w1_ref, index_ref, rank_ref, owner_ref = refs[KEPT : KEPT + 5]
+    kept_refs = refs[KEPT + 5 : 2 * KEPT + 5]
+    coords_ref, fracs_ref, pad, send, recv, load_sem, send_sem, recv_sem = refs[2 * KEPT + 5 :]
     me = lax.axis_index("brick")
     sources = (owner_hbm, coords_hbm, fracs_hbm) + kept_hbm
-    targets = (owner_ref, coords_ref, fracs_ref) + kept_refs
+    table = kept_refs[0]
+    cell_rows = kept_hbm[0].shape[0]
+    targets = (owner_ref, coords_ref, fracs_ref, table.at[:cell_rows]) + kept_refs[1:]
     loads = [
         pltpu.make_async_copy(a, b, load_sem.at[i]) for i, (a, b) in enumerate(zip(sources, targets))
     ]
@@ -126,40 +130,24 @@
         )
         copy.start()
         copies.append(copy)
-    for copy in copies:
-        copy.wait()
-
-    low = iota((n, LANES), 1) < HALF
-    ci = jnp.where(low, recv[:, 0, :], 0.0).astype(jnp.int32)
-    cj = jnp.where(low, recv[:, 1, :], 0.0).astype(jnp.int32)
-    base = ci * (BS * BS // LANES)
-    index_ref[:n] = base + (cj >> 1)
-    index_ref[n:] = base + ((cj + 1) >> 1)
-    got_ref[...] = recv[...]
-    for load in loads[3:]:
-        load.wait()
-
-
-def answer(
-    n, cap, index_ref, got_ref, rank_ref, owner_ref, cells, counts_ref, dist_ref, kernel_ref,
-    redist_ref, shatter_ref, out_ref,
-    index_s, wa0, wa1, wb0, wb1, stage_a, stage_b, rsend, rrecv, index_sem, rsend_sem, rrecv_sem,
-):
-    me = lax.axis_index("brick")
-    index_copy = pltpu.make_async_copy(index_ref, index_s, index_sem)
-    index_copy.start()
-    barrier = greet(me, n)
-    in_low = iota((n, LANES), 1) < HALF
+
+    loads[3].wait()
+    front = iota((CHUNK,) + table.shape[1:], 2) < HALF
+
+    def merge(i, carry):
+        at = i * CHUNK
+        here, after = table[pl.ds(at, CHUNK)], table[pl.ds(at + 1, CHUNK)]
+        table[pl.ds(cell_rows + at, CHUNK)] = jnp.where(front, after, here)
+        return carry
+
+    lax.fori_loop(0, cell_rows // CHUNK, merge, 0)
+
     lanes = iota((cap, LANES), 1)
     inner = (lanes % HALF).astype(jnp.float32)
     lower = lanes < HALF
-    plane = BS * BS // LANES
-    front = iota((3, LANES), 1) < HALF
-    ones = jnp.ones((8, 2 * LANES), jnp.bfloat16)
-    blank = jnp.zeros((1, HALF), jnp.float32)
-
-    def weigh(d, w0_ref, w1_ref):
-        block = got_ref[d]
+
+    def weigh(d):
+        block = recv[d]
         turned = pltpu.roll(block, HALF, 1)
         odd = (block.astype(jnp.int32) & 1) == 1
         even = jnp.where(odd, turned, 1.0 - turned)
@@ -170,21 +158,57 @@
         a2 = columns[HALF : HALF + cap, 2:3]
         w = jnp.where(inner == ck, 1.0 - a2, jnp.where(inner == ck + 1.0, a2, 0.0))
         w = w * jnp.where(lower, ae, 1.0 - ae)
-        w0_ref[...] = w * (1.0 - a0)
-        w1_ref[...] = w * a0
-
-    def gather(d, w0_ref, w1_ref, stage):
+        w0_ref[d * cap : (d + 1) * cap, :] = w * (1.0 - a0)
+        w1_ref[d * cap : (d + 1) * cap, :] = w * a0
+
+    order = [0]
+    for near in range(1, n // 2 + 1):
+        order += sorted({near, n - near})
+    for start in range(0, n, 4):
+        for d in order[start : start + 4]:
+            if d:
+                copies[d - 1].wait()
+        for d in order[start : start + 4]:
+            weigh(d)
+    low = iota((n, LANES), 1) < HALF
+    ci = jnp.where(low, recv[:, 0, :], 0.0).astype(jnp.int32)
+    cj = jnp.where(low, recv[:, 1, :], 0.0).astype(jnp.int32)
+    index_ref[...] = ci * (BS * BS // LANES) + (cj >> 1) + (cj & 1) * cell_rows
+    for load in loads[4:]:
+        load.wait()
+
+
+def answer(
+    n, cap, w0_ref, w1_ref, index_ref, rank_ref, owner_ref, table, counts_ref, dist_ref, kernel_ref,
+    redist_ref, shatter_ref, out_ref,
+    index_s, stage_a, stage_b, rsend, rrecv, index_sem, rsend_sem, rrecv_sem,
+):
+    me = lax.axis_index("brick")
+    index_copy = pltpu.make_async_copy(index_ref, index_s, index_sem)
+    index_copy.start()
+    barrier = greet(me, n)
+    in_low = iota((n, LANES), 1) < HALF
+    plane = BS * BS // LANES
+    ones = jnp.ones((8, 2 * LANES), jnp.bfloat16)
+
+    def gather(d, stage):
         for c in range(cap):
-            up = index_s[d, c]
-            dn = index_s[n + d, c]
-            near = jnp.where(front, cells[dn], cells[up])
-            far = jnp.where(front, cells[dn + plane], cells[up + plane])
-            acc = near * w0_ref[c : c + 1, :] + far * w1_ref[c : c + 1, :]
-            stage[pl.ds(c, 3, stride=HALF), :] = acc
+            at = index_s[d, c]
+            row = d * cap + c
+            stage[c] = (
+                table[at] * w0_ref[pl.ds(row, 1), :] + table[at + plane] * w1_ref[pl.ds(row, 1), :]
+            )
 
     def reduce(stage):
-        total = mxu(ones, jnp.concatenate(pieces(stage[...], 2), axis=1), NT)[:1]
-        return total[:, :LANES], jnp.concatenate([total[:, LANES:], blank], axis=1)
+        rows = []
+        for f in range(3):
+            rows.append(stage[:, f, :])
+            if cap < HALF:
+                rows.append(jnp.zeros((HALF - cap, LANES), jnp.float32))
+        rows.append(jnp.zeros((HALF, LANES), jnp.float32))
+        rows = jnp.concatenate(rows, axis=0)
+        total = mxu(ones, jnp.concatenate(pieces(rows, 2), axis=1), NT)[:1]
+        return total[:, :LANES], total[:, LANES:]
 
     def back(d):
         return pltpu.make_async_remote_copy(
@@ -200,27 +224,20 @@
         rsend[d, 0:1], rsend[d, 1:2] = reduce(stage)
         back(d).start()
 
-    if cap < HALF:
-        stage_a[...] = jnp.zeros_like(stage_a)
-        stage_b[...] = jnp.zeros_like(stage_b)
-    weigh(1, wa0, wa1)
     index_copy.wait()
-    gather(1, wa0, wa1, stage_a)
-    weigh(2, wb0, wb1)
+    gather(1, stage_a)
     pl.semaphore_wait(barrier, n - 1)
 
     def two(i, carry):
         d = 2 * i + 2
-        weigh(d + 1, wa0, wa1)
-        gather(d, wb0, wb1, stage_b)
+        gather(d, stage_b)
         finish(d - 1, stage_a)
-        weigh(lax.rem(d + 2, n), wb0, wb1)
-        gather(d + 1, wa0, wa1, stage_a)
+        gather(d + 1, stage_a)
         finish(d, stage_b)
         return carry
 
     lax.fori_loop(0, n // 2 - 1, two, 0)
-    gather(0, wb0, wb1, stage_b)
+    gather(0, stage_b)
     finish(n - 1, stage_a)
     rrecv[0, 0:1], rrecv[0, 1:2] = reduce(stage_b)
 
@@ -283,17 +300,20 @@
         counts.reshape(1, tracers), distribution, kernel, redist, shatter,
     )
     assert len(kept) == KEPT
-    got, index, rank, owner, *kept = pl.pallas_call(
-        functools.partial(request, n),
+    table = jax.ShapeDtypeStruct((2 * kept[0].shape[0], *kept[0].shape[1:]), f32)
+    w0, w1, index, rank, owner, *kept = pl.pallas_call(
+        functools.partial(request, n, cap),
         out_shape=(
-            jax.ShapeDtypeStruct((n, 4, LANES), f32),
-            jax.ShapeDtypeStruct((2 * n, LANES), jnp.int32),
+            jax.ShapeDtypeStruct((n * cap, LANES), f32),
+            jax.ShapeDtypeStruct((n * cap, LANES), f32),
+            jax.ShapeDtypeStruct((n, LANES), jnp.int32),
             jax.ShapeDtypeStruct((1, tracers), jnp.int32),
             jax.ShapeDtypeStruct((1, tracers), jnp.int32),
-            *[jax.ShapeDtypeStruct(x.shape, x.dtype) for x in kept],
+            table,
+            *[jax.ShapeDtypeStruct(x.shape, x.dtype) for x in kept[1:]],
         ),
         in_specs=[hbm] * (3 + KEPT),
-        out_specs=(vmem,) * (4 + KEPT),
+        out_specs=(vmem,) * (5 + KEPT),
         scratch_shapes=[
             pltpu.VMEM(coords.shape, jnp.int32),
             pltpu.VMEM(fracs.shape, f32),
@@ -312,12 +332,11 @@
     return pl.pallas_call(
         functools.partial(answer, n, cap),
         out_shape=jax.ShapeDtypeStruct((bins, tracers), f32),
-        in_specs=[vmem] * (4 + KEPT),
+        in_specs=[vmem] * (5 + KEPT),
         out_specs=vmem,
         scratch_shapes=[
-            pltpu.SMEM((2 * n, LANES), jnp.int32),
-            *[pltpu.VMEM((cap, LANES), f32)] * 4,
-            *[pltpu.VMEM((3 * HALF, LANES), f32)] * 2,
+            pltpu.SMEM((n, LANES), jnp.int32),
+            *[pltpu.VMEM((cap, 3, LANES), f32)] * 2,
             pltpu.VMEM((n, 2, LANES), f32),
             pltpu.VMEM((n, 2, LANES), f32),
             pltpu.SemaphoreType.DMA,
@@ -328,7 +347,7 @@
             collective_id=1, has_side_effects=True, vmem_limit_bytes=24 * 1024 * 1024
         ),
         name="answer",
-    )(index, got, rank, owner, *kept)
+    )(w0, w1, index, rank, owner, *kept)
 
 
 def solution(mesh):

time: 25 us -> 24.9 us (level)
    pallas_call x1, Pallas kernels: 14.8 us -> 11.4 us  [shards(): pl.pallas_call(functools.partial(answer, n, cap), out_shape=jax.ShapeDtyp...]
    pallas_call x1, Pallas kernels: 9.34 us -> 12.7 us  [shards(): pl.pallas_call(functools.partial(request, n, cap), out_shape=(jax.ShapeDt...]
where the time goes in v4:
time: 24.9 us; the launch traced here: 24.8 us
  Pallas kernels  24.1 us (97%)
  local copies, waits for them, and re-layouts  0.66 us (3%)
    pallas_call x1, Pallas kernels, shards(): pl.pallas_call(functools.partial(request, n, cap), out_shape=(jax.ShapeDt...  12.7 us
    pallas_call x1, Pallas kernels, shards(): pl.pallas_call(functools.partial(answer, n, cap), out_shape=jax.ShapeDtyp...  11.4 us
    unnamed x1, local copies, waits for them, and re-layouts  0.66 us

profile of v4, /device:TPU:0, one launch (start us, length us, event | category | flops | bytes accessed | tf_op | source)
XLA Modules:
  0.0 24.8 jit_solution(9497387557576561731)
XLA Ops:
  0.0 12.7 %request.1 = (f32[1024,128]{1,0:T(8,128)S(1)}, f32[1024,128]{1,0:T(8,128)S(1)}, s32[16,128]{1,0:T(8,128)S(1)}, s32[1,512]{1,0:T(1,128)S(1)}, s32[1,512]{1,0:T(1,...) custom-call(s32[1,512]{1,0:T(1,128)} %bitcast.6, ...), custom_call_target="tpu_custom_call" | custom-call | tf_op jit(solution)/shard_map/request/pallas_call | solution.py:304
  12.7 11.4 %answer.1 = f32[64,512]{1,0:T(8,128)S(1)} custom-call(f32[1024,128]{1,0:T(8,128)S(1)} %get-tuple-element.16.w0_ref, f32[1024,128]{1,0:T(8,128)S(1)} %get-tuple-element.17.w1_ref, s32[16,128]{1,0:T(8,128)S(1)} %get-tuple-element.18.index_ref, s32[1,512]{1,0:T(1,128)S(1)} %get-tuple-element.19.rank_ref, s32[1,512]{1,0:T(1,128)S(1)} %get-tuple-element.20.owner_ref, ...), custom_call_target="tpu_custom_call" | custom-call | tf_op jit(solution)/shard_map/answer/pallas_call | solution.py:332
  24.1 0.7 %copy.11 = f32[64,512]{1,0:T(8,128)} copy(f32[64,512]{1,0:T(8,128)S(1)} %answer.1) | data formatting | bytes 262144

commit v5 on v2

--- a/solution.py
+++ b/solution.py
@@ -181,20 +181,25 @@
             far = jnp.where(front, cells[dn + plane], cells[up + plane])
             at = s * cap + c
             acc = near * w0_ref[pl.ds(at, 1), :] + far * w1_ref[pl.ds(at, 1), :]
-            stage[pl.ds(s * 3 * HALF + c, 3, stride=HALF), :] = acc
+            stage[at] = acc
         return carry
 
-    ones = jnp.ones((8, LANES), jnp.bfloat16)
-    blank = jnp.zeros((1, HALF), jnp.float32)
+    ones = jnp.ones((8, 2 * LANES), jnp.bfloat16)
     size = n // GROUPS
     copies = []
     for g in range(GROUPS):
         lax.fori_loop(g * size, (g + 1) * size, one, 0)
         for s in range(g * size, (g + 1) * size):
-            block = stage[s * 3 * HALF : (s + 1) * 3 * HALF, :]
-            total = sum(mxu(ones, p, NT) for p in pieces(block))[:1]
+            rows = []
+            for f in range(3):
+                rows.append(stage[s * cap : (s + 1) * cap, f, :])
+                if cap < HALF:
+                    rows.append(jnp.zeros((HALF - cap, LANES), jnp.float32))
+            rows.append(jnp.zeros((HALF, LANES), jnp.float32))
+            rows = jnp.concatenate(pieces(jnp.concatenate(rows, axis=0), 2), axis=1)
+            total = mxu(ones, rows, NT)[:1]
             rsend[s, 0:1] = total[:, :LANES]
-            rsend[s, 1:2] = jnp.concatenate([total[:, LANES:], blank], axis=1)
+            rsend[s, 1:2] = total[:, LANES:]
         if g == 0:
             pl.semaphore_wait(barrier, n - 1)
             rrecv[0] = rsend[0]
@@ -304,7 +309,7 @@
         scratch_shapes=[
             pltpu.VMEM((n * cap, LANES), f32),
             pltpu.VMEM((n * cap, LANES), f32),
-            pltpu.VMEM((n * 3 * HALF, LANES), f32),
+            pltpu.VMEM((n * cap, 3, LANES), f32),
             pltpu.VMEM((n, 2, LANES), f32),
             pltpu.VMEM((n, 2, LANES), f32),
             pltpu.SemaphoreType.DMA((n,)),

time: 24 us -> 23.2 us (0.967)
  Pallas kernels: 23.2 us -> 22.4 us
    pallas_call x1, Pallas kernels: 13.9 us -> 13 us  [shards(): pl.pallas_call(functools.partial(answer, n, cap), out_shape=jax.ShapeDtyp...]
where the time goes in v5:
time: 23.2 us; the launch traced here: 23.1 us
  Pallas kernels  22.4 us (97%)
  local copies, waits for them, and re-layouts  0.66 us (3%)
    pallas_call x1, Pallas kernels, shards(): pl.pallas_call(functools.partial(answer, n, cap), out_shape=jax.ShapeDtyp...  13 us
    pallas_call x1, Pallas kernels, shards(): pl.pallas_call(functools.partial(request, n), out_shape=(jax.ShapeDtypeSt...  9.34 us
    unnamed x1, local copies, waits for them, and re-layouts  0.66 us

profile of v5, /device:TPU:0, one launch (start us, length us, event | category | flops | bytes accessed | tf_op | source)
XLA Modules:
  0.0 23.1 jit_solution(4013373226447729506)
XLA Ops:
  0.0 9.3 %request.1 = (f32[16,4,128]{2,1,0:T(4,128)S(1)}, s32[32,128]{1,0:T(8,128)S(1)}, s32[1,512]{1,0:T(1,128)S(1)}, s32[1,512]{1,0:T(1,128)S(1)}, f32[2048,3,128]{2,1,...) custom-call(s32[1,512]{1,0:T(1,128)} %bitcast.6, ...), custom_call_target="tpu_custom_call" | custom-call | tf_op jit(solution)/shard_map/request/pallas_call | solution.py:278
  9.3 13.0 %answer.1 = f32[64,512]{1,0:T(8,128)S(1)} custom-call(s32[32,128]{1,0:T(8,128)S(1)} %get-tuple-element.15.index_ref, f32[16,4,128]{2,1,0:T(4,128)S(1)} %get-tuple-element.16.got_ref, s32[1,512]{1,0:T(1,128)S(1)} %get-tuple-element.17.rank_ref, s32[1,512]{1,0:T(1,128)S(1)} %get-tuple-element.18.owner_ref, f32[2048,3,128]{2,1,0:T(4,128)S(1)} %get-tuple-element.19.cells, ...), custom_call_target="tpu_custom_call" | custom-call | tf_op jit(solution)/shard_map/answer/pallas_call | solution.py:304
  22.4 0.7 %copy.11 = f32[64,512]{1,0:T(8,128)} copy(f32[64,512]{1,0:T(8,128)S(1)} %answer.1) | data formatting | bytes 262144
